TPU v7x, 32 devices: a whole 2x2x4 slice. The times are simulated.
32 devices in a mesh: tm: 8 (over z, core), dp: 2 (over y), rep: 2 (over x).
Axes of the slice: x: 2, y: 2, z: 4, core: 2. Of those that a mesh axis runs over, the one named last changes fastest.
Arguments:
- clip_frames: bfloat16 [4, 32, 8, 4, 256], P(('dp', 'rep'), 'tm'), may hold values from -6 to 6
- conv_weight: bfloat16 [3, 3, 3, 256, 256], replicated, may hold values from -0.078125 to 0.078125
- up_weight: bfloat16 [256, 1024], replicated, may hold values from -0.375 to 0.375
- cotangent: bfloat16 [4, 32, 8, 4, 1024], P(('dp', 'rep'), None, 'tm'), may hold values from -6 to 6
Outputs:
- input_grad: bfloat16 [4, 32, 8, 4, 256], P(('dp', 'rep'), 'tm')
- up_grad: float32 [256, 1024], P('tm', ('dp', 'rep'))
All inputs are finite; a program needn't handle non-finite values.
Results may differ from a plain program's by a relative error of at most 0.012.
Values may be sent and summed in bfloat16 or wider, within the bound.
No kernel may reach another device: no remote copies, remote signals or barrier semaphores. Data moves between devices by JAX's collectives and lax.ppermute only.
A program may use at most 128 MiB of HBM per device.

v0:
```python
import math
import jax
import jax.numpy as jnp
from jax import lax
from jax.sharding import PartitionSpec as P


def from_behind(value, axis, steps):
    count = lax.axis_size(axis)
    initial, last = (max(0, -steps), min(count, count - steps))
    return lax.ppermute(value, axis, [(source, source + steps) for source in range(initial, last)])


def correlate(source, kernel, frames):
    rows = source.shape[1] - 2
    cols = source.shape[2] - 2
    patches = []
    for shift_t in range(3):
        for shift_r in range(3):
            for shift_c in range(3):
                patches.append(
                    source[
                        shift_t : shift_t + frames,
                        shift_r : shift_r + rows,
                        shift_c : shift_c + cols,
                    ]
                )
    stacked = jnp.concatenate(patches, axis=-1)
    width = stacked.shape[-1]
    flat_kernel = kernel.reshape(width, kernel.shape[-1])
    return jnp.dot(stacked.reshape(-1, width), flat_kernel, preferred_element_type=jnp.float32)


def pad_space(field):
    return jnp.pad(field, ((0, 0), (1, 1), (1, 1), (0, 0)))


def local(clip_frames, conv_weight, up_weight, cotangent):
    frames_local = clip_frames[0]
    frames = frames_local.shape[0]
    rows = frames_local.shape[1]
    cols = frames_local.shape[2]
    chans = frames_local.shape[3]
    is_first = lax.axis_index("tm") == 0
    earlier = from_behind(frames_local[frames - 2 :], "tm", 1)
    earlier = jnp.where(is_first, jnp.broadcast_to(frames_local[:1], earlier.shape), earlier)
    source = pad_space(jnp.concatenate([earlier, frames_local], axis=0))
    pre = correlate(source, conv_weight, frames)
    hidden = jax.nn.silu(pre).astype(jnp.bfloat16).reshape(1, frames, rows, cols, chans)
    contract_rows = (((0,), (0,)), ((), ()))
    contract_cols = (((1,), (1,)), ((), ()))
    frame_cot = lax.all_to_all(cotangent, "tm", split_axis=1, concat_axis=2, tiled=True)
    flat_g = frame_cot.reshape(-1, frame_cot.shape[-1])
    term = lax.dot_general(
        hidden.reshape(-1, chans), flat_g, contract_rows, preferred_element_type=jnp.float32
    )
    hidden_grad = lax.dot_general(
        flat_g, up_weight, contract_cols, preferred_element_type=jnp.float32
    ).astype(jnp.bfloat16)
    sigma = jax.nn.sigmoid(pre)
    slope = sigma * (1.0 + pre * (1.0 - sigma))
    pre_grad = (hidden_grad.astype(jnp.float32) * slope).astype(jnp.bfloat16)
    pre_grad = pre_grad.reshape(frames, rows, cols, chans)
    later = from_behind(pre_grad[:2], "tm", -1)
    back_kernel = jnp.transpose(conv_weight[::-1, ::-1, ::-1], (0, 1, 2, 4, 3))
    grad_source = pad_space(jnp.concatenate([pre_grad, later], axis=0))
    input_grad = correlate(grad_source, back_kernel, frames).reshape(frames, rows, cols, chans)

    def edge_term():
        start = jnp.concatenate(
            [jnp.zeros((2, rows, cols, chans), jnp.bfloat16), pre_grad[:2]], axis=0
        )
        parts = correlate(pad_space(start), back_kernel, 2).reshape(2, rows, cols, chans)
        return parts[0] + parts[1]

    def no_term():
        return jnp.zeros((rows, cols, chans), jnp.float32)

    edge = lax.cond(is_first, edge_term, no_term)
    input_grad = input_grad.at[0].add(edge)
    time_count = lax.axis_size("tm")
    clip_count = lax.axis_size(("dp", "rep"))
    factor = 1.0 / math.sqrt(clip_count * frames * time_count * rows * cols)
    part = lax.psum_scatter(term, "tm", scatter_dimension=0, tiled=True)
    summed = lax.psum_scatter(part, ("dp", "rep"), scatter_dimension=1, tiled=True)
    return (input_grad.astype(jnp.bfloat16)[None], summed * factor)


def solution(mesh):
    in_specs = (
        P(("dp", "rep"), "tm", None, None, None),
        P(),
        P(),
        P(("dp", "rep"), None, "tm", None, None),
    )
    out_specs = (P(("dp", "rep"), "tm", None, None, None), P("tm", ("dp", "rep")))
    return jax.shard_map(local, mesh=mesh, in_specs=in_specs, out_specs=out_specs, check_vma=False)
```

profile of v0, /device:TPU:0, one launch (start us, length us, event | category | flops | bytes accessed | tf_op | source)
XLA Modules:
  0.0 133.0 jit_solution(5692337568943609760)
XLA Ops:
  7.2 0.0 copy-start
  7.2 0.8 slice_bitcast_fusion
  8.0 2.4 %collective-permute-start = (bf16[2,8,4,256]{3,2,1,0:T(4,128)(2,1)S(1)}, bf16[2,8,4,256]{3,2,1,0:T(4,128)(2,1)S(1)}, u32[]{:S(2)}, u32[]{:S(2)}) collective-permute-start(bf16[2,8,4,256]{3,2,1,0:T(4,128)(2,1)S(1)} %slice_bitcast_fusion), channel_id=1, source_target_pairs={{0,4},{4,8},{8,12},{12,16},{16,20},{20,24},{24,28},{1,5},{5,9},{9,... | collective-permute-start | bytes 98312 | tf_op jit(solution)/shard_map/ppermute | solution.py:11
  10.4 6.2 %all-to-all-start = ((bf16[1,32,1,4,1024]{4,3,2,0,1:T(4,128)(2,1)}), bf16[1,32,1,4,1024]{4,3,2,0,1:T(4,128)(2,1)S(1)}, u32[]{:S(2)}, u32[]{:S(2)}) async-start(bf16[1,32,1,4,1024]{4,3,2,0,1:T(4,128)(2,1)} %bitcast.45), calls=%async_computation | async-start | bytes 524288 | tf_op jit(solution)/shard_map/all_to_all | solution.py:52
  16.6 0.0 reduce-scatter.3.cloned.1.call-start
  16.6 0.7 slice_bitcast_fusion.1
  17.4 6.1 %copy.24 = bf16[3,3,3,256,256]{3,4,2,1,0:T(8,128)(2,1)} copy(bf16[3,3,3,256,256]{4,3,2,1,0:T(8,128)(2,1)} %param.9) | data formatting | bytes 7077888 | tf_op args[1]
  23.5 4.2 %reverse_bitcast_fusion = bf16[3,3,3,256,256]{4,3,2,1,0:T(8,128)(2,1)} fusion(bf16[3,3,3,256,256]{3,4,2,1,0:T(8,128)(2,1)} %copy.24), kind=kLoop, calls=%fused_computation.180 | loop fusion | bytes 7077888 | tf_op jit(solution)/shard_map/transpose | solution.py:65
  27.7 0.0 copy-done.2
  27.7 4.1 %rev.3 = bf16[3,3,3,256,256]{3,4,2,1,0:T(8,128)(2,1)} reverse(bf16[3,3,3,256,256]{3,4,2,1,0:T(8,128)(2,1)} %copy.24), dimensions={0,1,2} | reverse | bytes 7077888 | tf_op jit(solution)/shard_map/rev | solution.py:65
  31.8 0.0 collective-permute-done
  31.8 0.1 pad_maximum_fusion
  31.9 1.3 pad_slice_fusion.48
  33.2 0.8 pad_slice_fusion.49
  34.0 0.1 fusion.5
  34.1 0.6 concatenate.77
  34.8 0.0 copy-start.3
  34.8 1.5 %concatenate.78 = bf16[128,256]{1,0:T(8,128)(2,1)} reshape(bf16[4,8,4,256]{3,2,1,0:T(4,128)(2,1)} %get-tuple-element.33) | data formatting | bytes 131072 | tf_op jit(solution)/shard_map/concatenate | solution.py:28
  36.3 1.5 %concatenate.79 = bf16[128,256]{1,0:T(8,128)(2,1)} reshape(bf16[4,8,4,256]{3,2,1,0:T(4,128)(2,1)} %get-tuple-element.34) | data formatting | bytes 131072 | tf_op jit(solution)/shard_map/concatenate | solution.py:28
  37.8 0.6 concatenate.80
  38.4 1.5 %concatenate.81 = bf16[128,256]{1,0:T(8,128)(2,1)} reshape(bf16[4,8,4,256]{3,2,1,0:T(4,128)(2,1)} %get-tuple-element.35) | data formatting | bytes 131072 | tf_op jit(solution)/shard_map/concatenate | solution.py:28
  39.9 1.5 %concatenate.82 = bf16[128,256]{1,0:T(8,128)(2,1)} reshape(bf16[4,8,4,256]{3,2,1,0:T(4,128)(2,1)} %get-tuple-element.36) | data formatting | bytes 131072 | tf_op jit(solution)/shard_map/concatenate | solution.py:28
  41.4 1.5 %concatenate.83 = bf16[128,256]{1,0:T(8,128)(2,1)} reshape(bf16[4,8,4,256]{3,2,1,0:T(4,128)(2,1)} %get-tuple-element.37) | data formatting | bytes 131072 | tf_op jit(solution)/shard_map/concatenate | solution.py:28
  42.9 1.5 %concatenate.84 = bf16[128,256]{1,0:T(8,128)(2,1)} reshape(bf16[4,8,4,256]{3,2,1,0:T(4,128)(2,1)} %get-tuple-element.38) | data formatting | bytes 131072 | tf_op jit(solution)/shard_map/concatenate | solution.py:28
  44.4 1.5 %concatenate.85 = bf16[128,256]{1,0:T(8,128)(2,1)} reshape(bf16[4,8,4,256]{3,2,1,0:T(4,128)(2,1)} %get-tuple-element.39) | data formatting | bytes 131072 | tf_op jit(solution)/shard_map/concatenate | solution.py:28
  45.9 0.6 concatenate.86
  46.5 0.6 concatenate.87
  47.4 0.9 concatenate.99
  48.3 0.0 copy-done.4
  48.3 0.0 copy-done.3
  48.4 0.9 concatenate.102
  49.2 0.8 constant_dynamic-update-slice_fusion.52
  50.1 0.8 constant_dynamic-update-slice_fusion.51
  50.9 0.8 constant_dynamic-update-slice_fusion.50
  51.8 0.8 constant_dynamic-update-slice_fusion.49
  52.6 0.8 constant_dynamic-update-slice_fusion.48
  53.4 0.8 constant_dynamic-update-slice_fusion.47
  54.3 0.8 constant_dynamic-update-slice_fusion.46
  55.1 0.8 constant_dynamic-update-slice_fusion.45
  56.0 0.8 constant_dynamic-update-slice_fusion.44
  56.8 0.8 constant_dynamic-update-slice_fusion.43
  57.7 0.8 constant_dynamic-update-slice_fusion.42
  58.7 2.6 %fusion.10 = f32[128,256]{1,0:T(8,128)S(1)} fusion(bf16[128,6912]{1,0:T(8,128)(2,1)S(1)} %constant_dynamic-update-slice_fusion.27, bf16[6912,256]{1,0:T(8,128)(2,1)} %bitcast.37), kind=kOutput, calls=%fused_computation.182 | convolution fusion | flops 452984832 | bytes 5439488 | tf_op jit(solution)/shard_map/dot_general | solution.py:31
  61.4 0.0 all-to-all-done
  61.4 0.1 copy.33
  61.5 0.1 reshape.116
  61.5 0.0 copy-done
  61.6 0.3 fusion.2
  61.9 1.3 fusion.3
  63.3 1.3 collective-permute-start.1
  64.6 0.0 reduce-scatter.3.cloned.1.call-update
  64.6 0.0 reduce-scatter.5.cloned.1.call-start
  64.6 4.0 %conditional.1 = (f32[1,8,4,256]{3,1,2,0:T(8,128)S(1)}) conditional(s32[]{:T(128)} %convert_element_type.26, () %tuple.20, (bf16[4,8,4,256]{3,2,1,0:T(4,128)(2,1)S(1)}, bf16[3,3,3,256,256]{4,3,2,1,0:T(8,128)(2,1)}) %tuple.21), branch_computations={%region_0.1_spmd, %region_1.2_spmd} | conditional | flops 226500608 | bytes 9175050 | solution.py:79
  65.7 0.2 reshape.110
  65.9 2.7 %fusion.9 = f32[64,256]{1,0:T(8,128)S(1)} fusion(bf16[64,6912]{1,0:T(8,128)(2,1)S(1)} %reshape.110, bf16[6912,256]{1,0:T(8,128)(2,1)} %bitcast.36), kind=kOutput, calls=%fused_computation.181 | convolution fusion | flops 226492416 | bytes 4489216 | tf_op jit(solution)/shard_map/cond/branch_1_fun/dot_general | solution.py:31
  68.7 0.0 collective-permute-done.1
  68.8 0.0 copy-start.1
  69.3 1.5 %copy-done.1 = bf16[3,3,3,256,256]{3,4,2,1,0:T(8,128)(2,1)S(1)} copy-done((bf16[3,3,3,256,256]{3,4,2,1,0:T(8,128)(2,1)S(1)}, bf16[3,3,3,256,256]{3,4,2,1,0:T(8,128)(2,1)}, u32[]{:S(2)}) %copy-start.1) | copy-done | bytes 3538968
  70.8 0.7 fusion.11
  71.5 28.2 %reduce-scatter.3.cloned.1.call-done = f32[32,1024]{1,0:T(8,128)} async-done(((f32[256,1024]{1,0:T(8,128)}), f32[32,1024]{1,0:T(8,128)}) %reduce-scatter.3.cloned.1.call-update) | async-done | bytes 131088 | tf_op jit(solution)/shard_map/reduce_scatter | solution.py:84
  99.7 0.0 reduce-scatter.5.cloned.1.call-update
  99.8 0.7 copy.26
  100.4 24.3 %reduce-scatter.5.cloned.1.call-done = f32[32,256]{1,0:T(8,128)} async-done(((f32[32,1024]{1,0:T(8,128)}), f32[32,256]{1,0:T(8,128)}) %reduce-scatter.5.cloned.1.call-update) | async-done | bytes 32784 | tf_op jit(solution)/shard_map/reduce_scatter | solution.py:85
  124.8 1.4 %broadcast_multiply_fusion = f32[32,256]{1,0:T(8,128)} fusion(f32[32,256]{1,0:T(8,128)} %reduce-scatter.5.cloned.1.call-done), kind=kLoop, calls=%fused_computation.177 | loop fusion | flops 8192 | bytes 65536 | tf_op jit(solution)/shard_map/mul | solution.py:86
  (100 shorter events, 1.8 us)
Async XLA Ops:
  7.2 54.4 %copy-start = (bf16[256,1024]{1,0:T(8,128)(2,1)S(1)}, bf16[256,1024]{1,0:T(8,128)(2,1)}, u32[]{:S(2)}) copy-start(bf16[256,1024]{1,0:T(8,128)(2,1)} %param.10) | copy-start | bytes 1572868
  8.0 23.8 %collective-permute-start = (bf16[2,8,4,256]{3,2,1,0:T(4,128)(2,1)S(1)}, bf16[2,8,4,256]{3,2,1,0:T(4,128)(2,1)S(1)}, u32[]{:S(2)}, u32[]{:S(2)}) collective-permute-start(bf16[2,8,4,256]{3,2,1,0:T(4,128)(2,1)S(1)} %slice_bitcast_fusion), channel_id=1, source_target_pairs={{0,4},{4,8},{8,12},{12,16},{16,20},{20,24},{24,28},{1,5},{5,9},{9,... | collective-permute-start | bytes 98312 | tf_op jit(solution)/shard_map/ppermute | solution.py:11
  10.4 50.9 %all-to-all-start = ((bf16[1,32,1,4,1024]{4,3,2,0,1:T(4,128)(2,1)}), bf16[1,32,1,4,1024]{4,3,2,0,1:T(4,128)(2,1)S(1)}, u32[]{:S(2)}, u32[]{:S(2)}) async-start(bf16[1,32,1,4,1024]{4,3,2,0,1:T(4,128)(2,1)} %bitcast.45), calls=%async_computation | async-start | bytes 524288 | tf_op jit(solution)/shard_map/all_to_all | solution.py:52
  16.6 83.1 %reduce-scatter.3.cloned.1.call-start = ((), (), s32[]{:S(2)}) async-start(), calls=%async_computation.3 | async-start | bytes 1179648 | tf_op jit(solution)/shard_map/reduce_scatter | solution.py:84
  23.5 4.2 %copy-start.2 = (bf16[1,4,8,4,256]{4,3,2,1,0:T(4,128)(2,1)S(1)}, bf16[1,4,8,4,256]{4,3,2,1,0:T(4,128)(2,1)}, u32[]{:S(2)}) copy-start(bf16[1,4,8,4,256]{4,3,2,1,0:T(4,128)(2,1)} %param.8) | copy-start | bytes 196612
  34.8 13.6 %copy-start.3 = (bf16[4,8,4,256]{3,2,1,0:T(4,128)(2,1)S(1)}, bf16[4,8,4,256]{3,2,1,0:T(4,128)(2,1)}, u32[]{:S(2)}) copy-start(bf16[4,8,4,256]{3,2,1,0:T(4,128)(2,1)} %get-tuple-element.50) | copy-start | bytes 196612
  38.4 9.9 %copy-start.4 = (bf16[4,8,4,256]{3,2,1,0:T(4,128)(2,1)S(1)}, bf16[4,8,4,256]{3,2,1,0:T(4,128)(2,1)}, u32[]{:S(2)}) copy-start(bf16[4,8,4,256]{3,2,1,0:T(4,128)(2,1)} %get-tuple-element.53) | copy-start | bytes 196612
  63.3 5.4 %collective-permute-start.1 = (bf16[2,8,4,256]{3,1,2,0:T(8,128)(2,1)S(1)}, bf16[2,8,4,256]{3,1,2,0:T(8,128)(2,1)S(1)}, u32[]{:S(2)}, u32[]{:S(2)}) collective-permute-start(bf16[2,8,4,256]{3,1,2,0:T(8,128)(2,1)S(1)} %copy.21), channel_id=1, source_target_pairs={{4,0},{8,4},{12,8},{16,12},{20,16},{24,20},{28,24},{5,1},{9,5},{13... | collective-permute-start | bytes 98312 | tf_op jit(solution)/shard_map/ppermute | solution.py:11
  64.6 60.2 %reduce-scatter.5.cloned.1.call-start = ((), (), s32[]{:S(2)}) async-start(), calls=%async_computation.4 | async-start | bytes 163840 | tf_op jit(solution)/shard_map/reduce_scatter | solution.py:85
  68.8 2.0 %copy-start.1 = (bf16[3,3,3,256,256]{3,4,2,1,0:T(8,128)(2,1)S(1)}, bf16[3,3,3,256,256]{3,4,2,1,0:T(8,128)(2,1)}, u32[]{:S(2)}) copy-start(bf16[3,3,3,256,256]{3,4,2,1,0:T(8,128)(2,1)} %rev.3) | copy-start | bytes 10616836
Sparse Core Ops, SparseCore 0:
  64.7 34.9 reduce-scatter.2
  102.4 22.2 reduce-scatter.4
where the time goes:
time: 135 us; the launch traced here: 133 us
  waiting for transfers between devices  52.6 us (39%)
  local copies, waits for them, and re-layouts  46.5 us (34%)
  between operations  14.6 us (11%)
  starting transfers between devices  9.93 us (7%)
  matrix products  7.64 us (6%)
  other arithmetic  1.54 us (1%)
    reduce_scatter x1, waiting for transfers between devices, local(): part = lax.psum_scatter(term, 'tm', scatter_dimension=0, tiled=True)  28.2 us
    reduce_scatter x1, waiting for transfers between devices, local(): lax.psum_scatter(part, ('dp', 'rep'), scatter_dimension=1, tiled=True)  24.3 us
    unnamed x65, local copies, waits for them, and re-layouts  18.1 us
    concatenate x30, local copies, waits for them, and re-layouts, correlate(): stacked = jnp.concatenate(patches, axis=-1)  15.1 us
    all_to_all x1, starting transfers between devices, local(): lax.all_to_all(cotangent, 'tm', split_axis=1, concat_axis=2, tiled=True)  6.16 us
    dot_general x3, matrix products, correlate(): jnp.dot(stacked.reshape(-1, width), flat_kernel, preferred_element_type=j...  6.01 us
    transpose x1, local copies, waits for them, and re-layouts, local(): back_kernel = jnp.transpose(conv_weight[::-1, ::-1, ::-1], (0, 1, 2, 4, 3))  4.21 us
    rev x1, local copies, waits for them, and re-layouts, local(): back_kernel = jnp.transpose(conv_weight[::-1, ::-1, ::-1], (0, 1, 2, 4, 3))  4.13 us
  transfers between devices with their start and end apart: 5, of which 2 were waited for; matrix products, arithmetic and copies ran while one was open for 38% of the time, Pallas kernels for 0%

commit v1 on v0

--- a/solution.py
+++ b/solution.py
@@ -49,7 +49,10 @@
     hidden = jax.nn.silu(pre).astype(jnp.bfloat16).reshape(1, frames, rows, cols, chans)
     contract_rows = (((0,), (0,)), ((), ()))
     contract_cols = (((1,), (1,)), ((), ()))
-    frame_cot = lax.all_to_all(cotangent, "tm", split_axis=1, concat_axis=2, tiled=True)
+    frame_cot = jnp.concatenate(
+        lax.all_to_all(jnp.stack(jnp.split(cotangent, lax.axis_size("tm"), axis=1)), "tm", 0, 0),
+        axis=2,
+    )
     flat_g = frame_cot.reshape(-1, frame_cot.shape[-1])
     term = lax.dot_general(
         hidden.reshape(-1, chans), flat_g, contract_rows, preferred_element_type=jnp.float32

time: 135 us -> 147 us (1.089)
  local copies, waits for them, and re-layouts: 46.5 us -> 58.3 us
    unnamed x65 -> x70, local copies, waits for them, and re-layouts: 18.1 us -> 27.6 us
    concatenate x30, local copies, waits for them, and re-layouts: 15.1 us -> 16.7 us  [correlate(): stacked = jnp.concatenate(patches, axis=-1)]
  transfers between devices with their start and end apart: 5 -> 5, of which waited for: 2 -> 2; matrix products, arithmetic and copies ran while one was open for 38% -> 43% of each run, Pallas kernels for 0% -> 0%
where the time goes in v1:
time: 147 us; the launch traced here: 145 us
  local copies, waits for them, and re-layouts  58.3 us (40%)
  waiting for transfers between devices  52.7 us (36%)
  between operations  14.6 us (10%)
  starting transfers between devices  9.91 us (7%)
  matrix products  7.63 us (5%)
  other arithmetic  1.54 us (1%)
    reduce_scatter x1, waiting for transfers between devices, local(): part = lax.psum_scatter(term, 'tm', scatter_dimension=0, tiled=True)  28.2 us
    unnamed x70, local copies, waits for them, and re-layouts  27.6 us
    reduce_scatter x1, waiting for transfers between devices, local(): lax.psum_scatter(part, ('dp', 'rep'), scatter_dimension=1, tiled=True)  24.4 us
    concatenate x30, local copies, waits for them, and re-layouts, correlate(): stacked = jnp.concatenate(patches, axis=-1)  16.7 us
    all_to_all x1, starting transfers between devices, local(): lax.all_to_all(jnp.stack(jnp.split(cotangent, lax.axis_size('tm'), axis=1...  6.15 us
    dot_general x3, matrix products, correlate(): jnp.dot(stacked.reshape(-1, width), flat_kernel, preferred_element_type=j...  6.01 us
    transpose x1, local copies, waits for them, and re-layouts, local(): back_kernel = jnp.transpose(conv_weight[::-1, ::-1, ::-1], (0, 1, 2, 4, 3))  4.2 us
    rev x1, local copies, waits for them, and re-layouts, local(): back_kernel = jnp.transpose(conv_weight[::-1, ::-1, ::-1], (0, 1, 2, 4, 3))  4.13 us
  transfers between devices with their start and end apart: 5, of which 2 were waited for; matrix products, arithmetic and copies ran while one was open for 43% of the time, Pallas kernels for 0%

profile of v1, /device:TPU:0, one launch (start us, length us, event | category | flops | bytes accessed | tf_op | source)
XLA Modules:
  0.0 144.8 jit_solution(3468411157536217187)
XLA Ops:
  7.2 0.0 copy-start
  7.2 0.8 slice_bitcast_fusion.7
  8.0 2.4 %collective-permute-start = (bf16[2,8,4,256]{3,2,1,0:T(4,128)(2,1)S(1)}, bf16[2,8,4,256]{3,2,1,0:T(4,128)(2,1)S(1)}, u32[]{:S(2)}, u32[]{:S(2)}) collective-permute-start(bf16[2,8,4,256]{3,2,1,0:T(4,128)(2,1)S(1)} %slice_bitcast_fusion.7), channel_id=1, source_target_pairs={{0,4},{4,8},{8,12},{12,16},{16,20},{20,24},{24,28},{1,5},{5,9},{9,... | collective-permute-start | bytes 98312 | tf_op jit(solution)/shard_map/ppermute | solution.py:11
  10.4 1.4 constant_dynamic-update-slice_fusion.34
  11.8 1.4 constant_dynamic-update-slice_fusion.33
  13.2 1.4 constant_dynamic-update-slice_fusion.32
  14.5 1.4 constant_dynamic-update-slice_fusion.31
  15.9 1.4 constant_dynamic-update-slice_fusion.30
  17.3 1.4 constant_dynamic-update-slice_fusion.29
  18.6 1.4 constant_dynamic-update-slice_fusion.28
  20.0 1.4 constant_dynamic-update-slice_fusion.27
  21.4 6.1 %all-to-all-start = ((bf16[8,1,4,1,4,1024]{5,4,2,3,1,0:T(4,128)(2,1)}), bf16[8,1,4,1,4,1024]{5,4,2,3,1,0:T(4,128)(2,1)S(1)}, u32[]{:S(2)}, u32[]{:S(2)}) async-start(bf16[8,1,4,1,4,1024]{5,4,2,3,1,0:T(4,128)(2,1)} %constant_dynamic-update-slice_fusion.27), calls=%async_computation | async-start | bytes 524288 | tf_op jit(solution)/shard_map/all_to_all | solution.py:53
  27.5 0.0 reduce-scatter.3.cloned.1.call-start
  27.6 0.7 slice_bitcast_fusion.8
  28.3 6.1 %copy.30 = bf16[3,3,3,256,256]{3,4,2,1,0:T(8,128)(2,1)} copy(bf16[3,3,3,256,256]{4,3,2,1,0:T(8,128)(2,1)} %param.9) | data formatting | bytes 7077888 | tf_op args[1]
  34.4 4.2 %reverse_bitcast_fusion = bf16[3,3,3,256,256]{4,3,2,1,0:T(8,128)(2,1)} fusion(bf16[3,3,3,256,256]{3,4,2,1,0:T(8,128)(2,1)} %copy.30), kind=kLoop, calls=%fused_computation.194 | loop fusion | bytes 7077888 | tf_op jit(solution)/shard_map/transpose | solution.py:68
  38.6 4.1 %rev.3 = bf16[3,3,3,256,256]{3,4,2,1,0:T(8,128)(2,1)} reverse(bf16[3,3,3,256,256]{3,4,2,1,0:T(8,128)(2,1)} %copy.30), dimensions={0,1,2} | reverse | bytes 7077888 | tf_op jit(solution)/shard_map/rev | solution.py:68
  42.7 0.0 collective-permute-done
  42.8 0.1 pad_maximum_fusion
  42.8 1.3 pad_slice_fusion.48
  44.1 0.2 pad_slice_fusion.49
  44.3 0.1 fusion.5
  44.4 0.6 concatenate.77
  45.1 1.5 %concatenate.78 = bf16[128,256]{1,0:T(8,128)(2,1)} reshape(bf16[4,8,4,256]{3,2,1,0:T(4,128)(2,1)} %get-tuple-element.31) | data formatting | bytes 131072 | tf_op jit(solution)/shard_map/concatenate | solution.py:28
  46.6 1.5 %concatenate.79 = bf16[128,256]{1,0:T(8,128)(2,1)} reshape(bf16[4,8,4,256]{3,2,1,0:T(4,128)(2,1)} %get-tuple-element.32) | data formatting | bytes 131072 | tf_op jit(solution)/shard_map/concatenate | solution.py:28
  48.0 0.6 concatenate.80
  48.7 1.5 %concatenate.81 = bf16[128,256]{1,0:T(8,128)(2,1)} reshape(bf16[4,8,4,256]{3,2,1,0:T(4,128)(2,1)} %get-tuple-element.33) | data formatting | bytes 131072 | tf_op jit(solution)/shard_map/concatenate | solution.py:28
  50.2 1.5 %concatenate.82 = bf16[128,256]{1,0:T(8,128)(2,1)} reshape(bf16[4,8,4,256]{3,2,1,0:T(4,128)(2,1)} %get-tuple-element.34) | data formatting | bytes 131072 | tf_op jit(solution)/shard_map/concatenate | solution.py:28
  51.6 1.5 %concatenate.83 = bf16[128,256]{1,0:T(8,128)(2,1)} reshape(bf16[4,8,4,256]{3,2,1,0:T(4,128)(2,1)} %get-tuple-element.35) | data formatting | bytes 131072 | tf_op jit(solution)/shard_map/concatenate | solution.py:28
  53.1 1.5 %concatenate.84 = bf16[128,256]{1,0:T(8,128)(2,1)} reshape(bf16[4,8,4,256]{3,2,1,0:T(4,128)(2,1)} %get-tuple-element.36) | data formatting | bytes 131072 | tf_op jit(solution)/shard_map/concatenate | solution.py:28
  54.6 1.5 %concatenate.85 = bf16[128,256]{1,0:T(8,128)(2,1)} reshape(bf16[4,8,4,256]{3,2,1,0:T(4,128)(2,1)} %get-tuple-element.37) | data formatting | bytes 131072 | tf_op jit(solution)/shard_map/concatenate | solution.py:28
  56.1 1.5 %concatenate.86 = bf16[128,256]{1,0:T(8,128)(2,1)} reshape(bf16[4,8,4,256]{3,2,1,0:T(4,128)(2,1)} %get-tuple-element.38) | data formatting | bytes 131072 | tf_op jit(solution)/shard_map/concatenate | solution.py:28
  57.5 1.5 %concatenate.87 = bf16[128,256]{1,0:T(8,128)(2,1)} reshape(bf16[4,8,4,256]{3,2,1,0:T(4,128)(2,1)} %get-tuple-element.39) | data formatting | bytes 131072 | tf_op jit(solution)/shard_map/concatenate | solution.py:28
  59.0 0.9 concatenate.88
  60.2 0.9 concatenate.102
  61.0 0.8 constant_dynamic-update-slice_fusion.60
  61.9 0.8 constant_dynamic-update-slice_fusion.59
  62.7 0.8 constant_dynamic-update-slice_fusion.58
  63.6 0.8 constant_dynamic-update-slice_fusion.57
  64.4 0.8 constant_dynamic-update-slice_fusion.56
  65.3 0.8 constant_dynamic-update-slice_fusion.55
  66.1 0.8 constant_dynamic-update-slice_fusion.54
  67.0 0.8 constant_dynamic-update-slice_fusion.53
  67.8 0.8 constant_dynamic-update-slice_fusion.52
  68.6 0.8 constant_dynamic-update-slice_fusion.51
  69.5 0.8 constant_dynamic-update-slice_fusion.50
  70.5 2.6 %fusion.10 = f32[128,256]{1,0:T(8,128)S(1)} fusion(bf16[128,6912]{1,0:T(8,128)(2,1)S(1)} %constant_dynamic-update-slice_fusion.35, bf16[6912,256]{1,0:T(8,128)(2,1)} %bitcast.70), kind=kOutput, calls=%fused_computation.196 | convolution fusion | flops 452984832 | bytes 5439488 | tf_op jit(solution)/shard_map/dot_general | solution.py:31
  73.2 0.1 copy.26
  73.3 0.1 reshape_reshape.3
  73.4 0.3 fusion.2
  73.7 1.3 fusion.3
  75.1 1.3 collective-permute-start.1
  76.4 0.0 reduce-scatter.3.cloned.1.call-update
  76.4 0.0 reduce-scatter.5.cloned.1.call-start
  76.5 4.0 %conditional.1 = (f32[1,8,4,256]{3,1,2,0:T(8,128)S(1)}) conditional(s32[]{:T(128)} %convert_element_type.26, () %tuple.20, (bf16[4,8,4,256]{3,2,1,0:T(4,128)(2,1)S(1)}, bf16[3,3,3,256,256]{4,3,2,1,0:T(8,128)(2,1)}) %tuple.21), branch_computations={%region_0.1_spmd, %region_1.2_spmd} | conditional | flops 226500608 | bytes 9175050 | solution.py:82
  77.5 0.2 reshape.109
  77.7 2.7 %fusion.9 = f32[64,256]{1,0:T(8,128)S(1)} fusion(bf16[64,6912]{1,0:T(8,128)(2,1)S(1)} %reshape.109, bf16[6912,256]{1,0:T(8,128)(2,1)} %bitcast.69), kind=kOutput, calls=%fused_computation.195 | convolution fusion | flops 226492416 | bytes 4489216 | tf_op jit(solution)/shard_map/cond/branch_1_fun/dot_general | solution.py:31
  81.1 1.5 %copy-done.1 = bf16[3,3,3,256,256]{3,4,2,1,0:T(8,128)(2,1)S(1)} copy-done((bf16[3,3,3,256,256]{3,4,2,1,0:T(8,128)(2,1)S(1)}, bf16[3,3,3,256,256]{3,4,2,1,0:T(8,128)(2,1)}, u32[]{:S(2)}) %copy-start.1) | copy-done | bytes 3538968
  82.6 0.7 fusion.11
  83.3 28.2 %reduce-scatter.3.cloned.1.call-done = f32[32,1024]{1,0:T(8,128)} async-done(((f32[256,1024]{1,0:T(8,128)}), f32[32,1024]{1,0:T(8,128)}) %reduce-scatter.3.cloned.1.call-update) | async-done | bytes 131088 | tf_op jit(solution)/shard_map/reduce_scatter | solution.py:87
  111.5 0.0 reduce-scatter.5.cloned.1.call-update
  111.5 0.7 copy.32
  112.2 24.4 %reduce-scatter.5.cloned.1.call-done = f32[32,256]{1,0:T(8,128)} async-done(((f32[32,1024]{1,0:T(8,128)}), f32[32,256]{1,0:T(8,128)}) %reduce-scatter.5.cloned.1.call-update) | async-done | bytes 32784 | tf_op jit(solution)/shard_map/reduce_scatter | solution.py:88
  136.6 1.4 broadcast_multiply_fusion
  (106 shorter events, 1.8 us)
Async XLA Ops:
  7.2 66.2 %copy-start = (bf16[256,1024]{1,0:T(8,128)(2,1)S(1)}, bf16[256,1024]{1,0:T(8,128)(2,1)}, u32[]{:S(2)}) copy-start(bf16[256,1024]{1,0:T(8,128)(2,1)} %param.10) | copy-start | bytes 1572868
  8.0 34.7 %collective-permute-start = (bf16[2,8,4,256]{3,2,1,0:T(4,128)(2,1)S(1)}, bf16[2,8,4,256]{3,2,1,0:T(4,128)(2,1)S(1)}, u32[]{:S(2)}, u32[]{:S(2)}) collective-permute-start(bf16[2,8,4,256]{3,2,1,0:T(4,128)(2,1)S(1)} %slice_bitcast_fusion.7), channel_id=1, source_target_pairs={{0,4},{4,8},{8,12},{12,16},{16,20},{20,24},{24,28},{1,5},{5,9},{9,... | collective-permute-start | bytes 98312 | tf_op jit(solution)/shard_map/ppermute | solution.py:11
  21.4 51.8 %all-to-all-start = ((bf16[8,1,4,1,4,1024]{5,4,2,3,1,0:T(4,128)(2,1)}), bf16[8,1,4,1,4,1024]{5,4,2,3,1,0:T(4,128)(2,1)S(1)}, u32[]{:S(2)}, u32[]{:S(2)}) async-start(bf16[8,1,4,1,4,1024]{5,4,2,3,1,0:T(4,128)(2,1)} %constant_dynamic-update-slice_fusion.27), calls=%async_computation | async-start | bytes 524288 | tf_op jit(solution)/shard_map/all_to_all | solution.py:53
  27.5 83.9 %reduce-scatter.3.cloned.1.call-start = ((), (), s32[]{:S(2)}) async-start(), calls=%async_computation.3 | async-start | bytes 1179648 | tf_op jit(solution)/shard_map/reduce_scatter | solution.py:87
  34.4 4.2 %copy-start.2 = (bf16[1,4,8,4,256]{4,3,2,1,0:T(4,128)(2,1)S(1)}, bf16[1,4,8,4,256]{4,3,2,1,0:T(4,128)(2,1)}, u32[]{:S(2)}) copy-start(bf16[1,4,8,4,256]{4,3,2,1,0:T(4,128)(2,1)} %param.8) | copy-start | bytes 196612
  45.0 15.0 %copy-start.3 = (bf16[4,8,4,256]{3,2,1,0:T(4,128)(2,1)S(1)}, bf16[4,8,4,256]{3,2,1,0:T(4,128)(2,1)}, u32[]{:S(2)}) copy-start(bf16[4,8,4,256]{3,2,1,0:T(4,128)(2,1)} %get-tuple-element.47) | copy-start | bytes 196612
  75.1 5.4 %collective-permute-start.1 = (bf16[2,8,4,256]{3,1,2,0:T(8,128)(2,1)S(1)}, bf16[2,8,4,256]{3,1,2,0:T(8,128)(2,1)S(1)}, u32[]{:S(2)}, u32[]{:S(2)}) collective-permute-start(bf16[2,8,4,256]{3,1,2,0:T(8,128)(2,1)S(1)} %copy.27), channel_id=1, source_target_pairs={{4,0},{8,4},{12,8},{16,12},{20,16},{24,20},{28,24},{5,1},{9,5},{13... | collective-permute-start | bytes 98312 | tf_op jit(solution)/shard_map/ppermute | solution.py:11
  76.4 60.2 %reduce-scatter.5.cloned.1.call-start = ((), (), s32[]{:S(2)}) async-start(), calls=%async_computation.4 | async-start | bytes 163840 | tf_op jit(solution)/shard_map/reduce_scatter | solution.py:88
  80.6 2.0 %copy-start.1 = (bf16[3,3,3,256,256]{3,4,2,1,0:T(8,128)(2,1)S(1)}, bf16[3,3,3,256,256]{3,4,2,1,0:T(8,128)(2,1)}, u32[]{:S(2)}) copy-start(bf16[3,3,3,256,256]{3,4,2,1,0:T(8,128)(2,1)} %rev.3) | copy-start | bytes 10616836
Sparse Core Ops, SparseCore 0:
  76.5 34.8 reduce-scatter.2
  114.2 22.3 reduce-scatter.4
